TPU v7x, 32 devices: a whole 2x2x4 slice. The times are simulated.
32 devices in a mesh: dp: 16 (over z, x, core), fsdp: 2 (over y).
Axes of the slice: x: 2, y: 2, z: 4, core: 2. Of those that a mesh axis runs over, the one named last changes fastest.
Arguments:
- grads: bfloat16 [16, 2, 8192, 1024], P('dp', None, 'fsdp'), may hold values from -1.1953125 to 1.1953125
- raw_proj: float32 [2, 1024, 512], P(None, 'fsdp'), may hold values from -6 to 6
- bucket_owner: int32 [2, 512], P(None, 'fsdp'), may hold values from 0 to 15, as said below
- first_moment: float32 [2, 2, 512, 16, 512], P(None, 'fsdp', 'dp'), may hold values from -0.6 to 0.6
- second_moment: float32 [2, 2, 512, 16, 512], P(None, 'fsdp', 'dp'), may hold values from 0.01 to 0.05
Outputs:
- weight_delta: bfloat16 [2, 8192, 1024], P(None, 'fsdp')
- first_out: float32 [2, 2, 512, 16, 512], P(None, 'fsdp', 'dp')
- second_out: float32 [2, 2, 512, 16, 512], P(None, 'fsdp', 'dp')
Inputs may be any that keep to these rules, and one draw needn't show every extreme that they name: `bucket_owner`: within each matrix and each block of 256 buckets of one fsdp index, no owner holds more than 32 buckets, and one owner holds exactly 32.
All inputs are finite; a program needn't handle non-finite values.
Results may differ from a plain program's by a relative error of at most 0.0062.
Values may be sent and summed in bfloat16 or wider, within the bound.
No kernel may reach another device: no remote copies, remote signals or barrier semaphores. Data moves between devices by JAX's collectives and lax.ppermute only.
A program may use at most 128 MiB of HBM per device.

v0:
```python
import jax
import jax.numpy as jnp
from jax import lax
from jax.sharding import PartitionSpec as P


def cholesky_basis(raw_rows):
    gram = jnp.einsum("mkr,mks->mrs", raw_rows, raw_rows, precision=lax.Precision.HIGHEST)
    factor = jnp.linalg.cholesky(gram)
    basis = lax.linalg.triangular_solve(
        factor, raw_rows, left_side=False, lower=True, transpose_a=True
    )
    return basis.astype(jnp.bfloat16)


def rows_at(table, index):
    return jax.vmap(lambda part_table, part_index: jnp.take(part_table, part_index, axis=0))(
        table, index
    )


def adam_update(first, second, grad_rows):
    new_first = 0.9 * first + 0.1 * grad_rows
    new_second = 0.999 * second + 0.001 * grad_rows * grad_rows
    scaled = (
        6.0 * (new_first / (1.0 - 0.9**10)) / (jnp.sqrt(new_second / (1.0 - 0.999**10)) + 1e-08)
    )
    return (new_first, new_second, scaled.astype(jnp.bfloat16))


def shards(grads, raw_proj, bucket_owner, first_moment, second_moment):
    matrices = grads.shape[1]
    local_rows = grads.shape[2]
    features = grads.shape[3]
    rank_width = raw_proj.shape[2]
    buckets = bucket_owner.shape[1]
    capacity = first_moment.shape[2]
    bucket_rows = local_rows // buckets
    replicas = lax.axis_size("dp")
    slot_total = replicas * capacity
    raw_whole = lax.all_gather(raw_proj, "fsdp", axis=1, tiled=True)
    basis = cholesky_basis(raw_whole)
    projected = jnp.einsum("mdk,mkr->mdr", grads[0], basis, preferred_element_type=jnp.float32)
    blocks = projected.reshape(matrices, buckets, bucket_rows, rank_width)
    same = bucket_owner[:, :, None] == bucket_owner[:, None, :]
    earlier = jnp.arange(buckets)[None, :] < jnp.arange(buckets)[:, None]
    ranks = jnp.sum(jnp.logical_and(same, earlier).astype(jnp.int32), axis=-1)
    slots = bucket_owner * capacity + ranks
    slot_ids = jnp.arange(slot_total, dtype=jnp.int32)
    matches = slots[:, None, :] == slot_ids[None, :, None]
    occupied = jnp.any(matches, axis=2)
    bucket_of = jnp.sum(
        matches.astype(jnp.int32) * jnp.arange(buckets, dtype=jnp.int32)[None, None, :], axis=2
    )
    start = lax.axis_index("dp") * capacity
    occupied_mine = lax.dynamic_slice_in_dim(occupied, start, capacity, 1)
    totals = lax.psum(blocks, "dp")
    bucket_mine = lax.dynamic_slice_in_dim(bucket_of, start, capacity, 1)
    grad_rows = rows_at(totals, bucket_mine)
    first = first_moment[:, 0]
    second = second_moment[:, 0]
    new_first, new_second, update = adam_update(first, second, grad_rows)
    keep_mask = occupied_mine[:, :, None, None]
    first_out = jnp.where(keep_mask, new_first, first)[:, None]
    second_out = jnp.where(keep_mask, new_second, second)[:, None]
    owner_rows = jnp.einsum(
        "mcbr,mkr->mcbk", update, basis, preferred_element_type=jnp.float32
    ).astype(jnp.bfloat16)
    every_rows = lax.all_gather(owner_rows, "dp", axis=1, tiled=True)
    delta = rows_at(every_rows, slots)
    weight_delta = delta.reshape(matrices, local_rows, features)
    return (weight_delta, first_out, second_out)


def solution(mesh):
    return jax.shard_map(
        shards,
        mesh=mesh,
        in_specs=(
            P("dp", None, "fsdp", None),
            P(None, "fsdp", None),
            P(None, "fsdp"),
            P(None, "fsdp", "dp", None, None),
            P(None, "fsdp", "dp", None, None),
        ),
        out_specs=(
            P(None, "fsdp", None),
            P(None, "fsdp", "dp", None, None),
            P(None, "fsdp", "dp", None, None),
        ),
        check_vma=False,
    )
```

profile of v0, /device:TPU:0, one launch (start us, length us, event | category | flops | bytes accessed | tf_op | source)
XLA Modules:
  0.0 912.8 jit_solution(13128395138361533035)
XLA Ops:
  7.2 0.7 all-gather.3.cloned.1.call-update
  8.0 0.1 iota_compare_fusion
  8.1 60.9 %all-gather.3.cloned.1.call-done = f32[2,1024,512]{2,1,0:T(8,128)} async-done(((f32[2,512,512]{2,1,0:T(8,128)}), f32[2,1024,512]{2,1,0:T(8,128)}) %all-gather.3.cloned.1.call-update) | async-done | bytes 4194320 | tf_op jit(solution)/shard_map/all_gather | solution.py:41
  69.0 10.4 %fusion.81 = f32[2,512,512]{2,1,0:T(8,128)S(1)} fusion(f32[2,1024,512]{2,1,0:T(8,128)} %all-gather.3.cloned.1.call-done), kind=kOutput, calls=%fused_computation.130 | convolution fusion | flops 6442450944 | bytes 6291456 | tf_op jit(solution)/shard_map/mkr,mks->mrs/dot_general | solution.py:8
  79.4 1.8 copy.45
  81.2 2.1 fusion.24
  83.3 1.3 copy-done.1
  84.6 23.5 %custom-call.34 = f32[2,128,128]{2,1,0:T(8,128)S(1)} custom-call(f32[2,128,128]{2,1,0:T(8,128)S(1)} %cholesky.274), custom_call_target="Cholesky" | custom-call | tf_op jit(solution)/shard_map/jit(cholesky)/cholesky | solution.py:9
  108.1 19.7 %custom-call.35 = f32[2,1,128,128]{2,3,1,0:T(8,128)S(1)} custom-call(f32[2,1,128,128]{3,2,1,0:T(8,128)S(1)} %select_bitcast_fusion.2), custom_call_target="InvertDiagBlocksLowerTriangular" | custom-call | tf_op jit(solution)/shard_map/jit(cholesky)/cholesky | solution.py:9
  127.8 0.3 cholesky.234
  128.1 1.5 constant_dynamic-update-slice_fusion.3
  129.6 1.5 convolution_subtract_fusion.1
  131.1 23.7 %custom-call.36 = f32[2,128,128]{2,1,0:T(8,128)S(1)} custom-call(f32[2,128,128]{2,1,0:T(8,128)S(1)} %cholesky.278), custom_call_target="Cholesky" | custom-call | tf_op jit(solution)/shard_map/jit(cholesky)/cholesky | solution.py:9
  154.8 19.7 %custom-call.37 = f32[2,1,128,128]{2,3,1,0:T(8,128)S(1)} custom-call(f32[2,1,128,128]{3,2,1,0:T(8,128)S(1)} %get-tuple-element.32), custom_call_target="InvertDiagBlocksLowerTriangular" | custom-call | tf_op jit(solution)/shard_map/jit(cholesky)/cholesky | solution.py:9
  174.5 0.4 convolution_dynamic-update-slice_fusion
  174.9 1.6 convolution_subtract_fusion.2
  176.4 23.5 %custom-call.38 = f32[2,128,128]{2,1,0:T(8,128)S(1)} custom-call(f32[2,128,128]{2,1,0:T(8,128)S(1)} %cholesky.283), custom_call_target="Cholesky" | custom-call | tf_op jit(solution)/shard_map/jit(cholesky)/cholesky | solution.py:9
  199.9 20.1 %custom-call.39 = f32[2,1,128,128]{2,3,1,0:T(8,128)S(1)} custom-call(f32[2,1,128,128]{3,2,1,0:T(8,128)S(1)} %get-tuple-element.30), custom_call_target="InvertDiagBlocksLowerTriangular" | custom-call | tf_op jit(solution)/shard_map/jit(cholesky)/cholesky | solution.py:9
  220.0 0.3 convolution_dynamic-update-slice_fusion.1
  220.3 1.5 convolution_subtract_fusion.3
  221.8 23.5 %custom-call.40 = f32[2,128,128]{2,1,0:T(8,128)S(1)} custom-call(f32[2,128,128]{2,1,0:T(8,128)S(1)} %convolution_subtract_fusion.3), custom_call_target="Cholesky" | custom-call | tf_op jit(solution)/shard_map/jit(cholesky)/cholesky | solution.py:9
  245.3 0.1 compare_reduce_fusion.2
  245.5 0.2 compare_reduce_fusion
  245.7 1.7 select_select_fusion
  247.4 14.2 %while.1 = (s32[]{:T(128)}, f32[2,512,512]{2,1,0:T(8,128)}, s32[4,2]{0,1:T(2,128)S(1)}, f32[4,2,128,128]{3,2,0,1:T(8,128)}, s32[]{:T(128)}) while((s32[]{:T(128)}, f32[2,512,512]{2,1,0:T(8,128)}, s32[4,2]{0,1:T(2,128)S(1)}, f32[4,2,128,128]{3,2,0,1:T(8,128)}, s32[]{:T(128)}) %tuple.37), condition=%wide.while_cond, body=%wide.while_body.sunk | while | flops 2 | bytes 263777 | solution.py:10
  247.4 0.1 constant_dynamic-slice_fusion.4
  247.5 0.5 fusion.90
  248.0 3.0 bitcast_dynamic-update-slice_fusion.2
  251.0 0.1 constant_dynamic-slice_fusion.4
  251.1 0.5 fusion.90
  251.6 3.0 bitcast_dynamic-update-slice_fusion.2
  254.6 0.1 constant_dynamic-slice_fusion.4
  254.6 0.5 fusion.90
  255.2 3.0 bitcast_dynamic-update-slice_fusion.2
  258.1 0.1 constant_dynamic-slice_fusion.4
  258.2 0.5 fusion.90
  258.8 2.9 bitcast_dynamic-update-slice_fusion.2
  261.7 79.6 %custom-call.41 = f32[2,4,128,128]{2,3,1,0:T(8,128)S(1)} custom-call(f32[2,4,128,128]{3,2,1,0:T(8,128)} %bitcast.133), custom_call_target="InvertDiagBlocksLowerTriangular" | custom-call | tf_op jit(solution)/shard_map/triangular_solve | solution.py:10
  341.3 2.3 bitcast_convert_fusion
  343.6 3.2 convolution_subtract_fusion
  346.8 1.1 fusion.80
  347.9 4.6 fusion.30
  352.5 1.1 fusion.79
  353.6 6.5 fusion.33
  360.2 1.1 convolution_convert_fusion
  361.3 15.9 %fusion.2 = f32[2,4096,512]{1,2,0:T(8,128)} fusion(bf16[1,2,4096,1024]{3,2,1,0:T(8,128)(2,1)} %param.5, bf16[2,1024,128]{1,2,0:T(8,128)(2,1)S(1)} %convolution_convert_fusion, bf16[2,1024,128]{1,2,0:T(8,128)(2,1)S(1)} %get-tuple-element.36, bf16[2,1024,128]{1,2,0:T(8,128)(2,1)S(1)} %get-tuple-element.38, bf16[2,1024,128]{1,2,0:T(8,128)(2,1)S(1)} %get-tuple-element.40), kind=kOutput, calls=%fused_computation.7 | convolution fusion | flops 8598323200 | bytes 35651584 | tf_op jit(solution)/shard_map/mdk,mkr->mdr/dot_general | solution.py:43
  377.2 17.5 %copy.60 = f32[2,4096,512]{2,1,0:T(8,128)} copy(f32[2,4096,512]{1,2,0:T(8,128)} %fusion.2) | data formatting | bytes 33554432 | tf_op jit(solution)/shard_map/mdk,mkr->mdr/dot_general | solution.py:43
  394.8 0.6 copy-done.4
  395.3 0.2 convert_reduce_fusion
  395.6 0.2 select_reduce_fusion
  395.8 0.1 bitcast_or_fusion.1
  395.9 0.1 reshape.134
  396.0 0.1 compare_and_fusion.1
  396.1 296.7 %all-reduce.3.cloned.1.call-done = f32[2,256,16,512]{3,2,1,0:T(8,128)} async-done(((f32[2,256,16,512]{3,2,1,0:T(8,128)}), f32[2,256,16,512]{3,2,1,0:T(8,128)}) %all-reduce.3.cloned.1.call-update) | async-done | bytes 16777232 | tf_op jit(solution)/shard_map/psum | solution.py:57
  692.8 6.5 gather_fusion
  699.3 6.2 fusion.27
  705.5 0.1 broadcast_in_dim.58
  705.7 0.2 broadcast_in_dim.59
  705.8 0.2 fusion.46
  706.1 0.1 constant_dynamic-slice_fusion.1
  706.1 5.2 fusion.17
  711.4 161.9 %all-gather.5.cloned.1.call-done = bf16[2,512,16,1024]{3,2,1,0:T(8,128)(2,1)} async-done(((bf16[2,32,16,1024]{3,2,1,0:T(8,128)(2,1)}), bf16[2,512,16,1024]{3,2,1,0:T(8,128)(2,1)}) %all-gather.5.cloned.1.call-update) | async-done | bytes 33554448 | tf_op jit(solution)/shard_map/all_gather | solution.py:69
  873.3 18.4 %gather_fusion.1 = bf16[512,16,1024]{2,1,0:T(8,128)(2,1)} fusion(bf16[2,512,16,1024]{3,2,1,0:T(8,128)(2,1)} %all-gather.5.cloned.1.call-done, s32[512]{0:T(512)S(1)} %bitcast.128), kind=kCustom, calls=%fused_computation.1 | custom fusion | bytes 33558528 | tf_op jit(solution)/shard_map/vmap(jit(_take))/gather | solution.py:17
  891.7 14.2 %bitcast_select_fusion = bf16[2,4096,1024]{2,1,0:T(8,128)(2,1)} fusion(pred[2,4096]{1,0:T(4,128)(4,1)S(1)} %broadcast_in_dim.59, bf16[2,4096,1024]{2,1,0:T(8,128)(2,1)} %bitcast.127), kind=kLoop, calls=%fused_computation.4 | loop fusion | flops 8388608 | bytes 33562624 | tf_op jit(solution)/shard_map/vmap(jit(_take))/select_n | solution.py:17
  (30 shorter events, 0.4 us)
Async XLA Ops:
  7.2 61.8 %all-gather.3.cloned.1.call-start = ((), (), s32[]{:S(2)}) async-start(), calls=%async_computation | async-start | bytes 6291456 | tf_op jit(solution)/shard_map/all_gather | solution.py:41
  7.9 684.9 %all-reduce.3.cloned.1.call-start = ((), (), s32[]{:S(2)}) async-start(), calls=%async_computation.1 | async-start | bytes 33554432 | tf_op jit(solution)/shard_map/psum | solution.py:57
  83.3 1.3 copy-start.1
  343.5 4.4 copy-start
  347.9 13.4 %copy-start.2 = (bf16[2,1024,128]{1,2,0:T(8,128)(2,1)}, bf16[2,1024,128]{1,2,0:T(8,128)(2,1)S(1)}, u32[]{:S(2)}) copy-start(bf16[2,1024,128]{1,2,0:T(8,128)(2,1)S(1)} %get-tuple-element.38) | copy-start | bytes 1572868
  353.6 7.7 copy-start.3
  394.7 0.7 copy-start.4
  394.7 478.6 %all-gather.5.cloned.1.call-start = ((), (), s32[]{:S(2)}) async-start(), calls=%async_computation.2 | async-start | bytes 35651584 | tf_op jit(solution)/shard_map/all_gather | solution.py:69
Sparse Core Ops, SparseCore 0:
  9.5 59.4 all-gather.2
  394.8 297.9 all-reduce.2
  705.6 167.6 all-gather.4
where the time goes:
time: 923 us; the launch traced here: 913 us
  waiting for transfers between devices  520 us (56%)
  other arithmetic  258 us (28%)
  local copies, waits for them, and re-layouts  61 us (7%)
  matrix products  59.1 us (6%)
  between operations  14.5 us (2%)
    psum x1, waiting for transfers between devices, shards(): totals = lax.psum(blocks, 'dp')  297 us
    all_gather x1, waiting for transfers between devices, shards(): every_rows = lax.all_gather(owner_rows, 'dp', axis=1, tiled=True)  162 us
    another operation x16, other arithmetic, cholesky_basis(): factor = jnp.linalg.cholesky(gram)  154 us
    another operation x4, other arithmetic, cholesky_basis(): lax.linalg.triangular_solve(factor, raw_rows, left_side=False, lower=True...  81.4 us
    all_gather x1, waiting for transfers between devices, shards(): raw_whole = lax.all_gather(raw_proj, 'fsdp', axis=1, tiled=True)  60.9 us
    gather x3, local copies, waits for them, and re-layouts, rows_at(): jnp.take(part_table, part_index, axis=0)  24.9 us
    another operation x7, matrix products, cholesky_basis(): lax.linalg.triangular_solve(factor, raw_rows, left_side=False, lower=True...  19.9 us
  transfers between devices with their start and end apart: 3, of which 3 were waited for; matrix products, arithmetic and copies ran while one was open for 1% of the time, Pallas kernels for 0%

commit v1 on v0

--- a/solution.py
+++ b/solution.py
@@ -54,7 +54,9 @@
     )
     start = lax.axis_index("dp") * capacity
     occupied_mine = lax.dynamic_slice_in_dim(occupied, start, capacity, 1)
-    totals = lax.psum(blocks, "dp")
+    totals = blocks
+    for hop in (1, 2, 4, 8):
+        totals = totals + lax.ppermute(totals, "dp", [(dev, dev ^ hop) for dev in range(16)])
     bucket_mine = lax.dynamic_slice_in_dim(bucket_of, start, capacity, 1)
     grad_rows = rows_at(totals, bucket_mine)
     first = first_moment[:, 0]

time: 923 us -> 2150 us (2.33)
  waiting for transfers between devices: 520 us -> 1690 us
  other arithmetic: 258 us -> 313 us
    ppermute x0 -> x4, waiting for transfers between devices: none -> 1460 us  [shards(): lax.ppermute(totals, 'dp', [(dev, dev ^ hop) for dev in range(16)])]
    psum x1 -> x0, waiting for transfers between devices: 297 us -> none  [shards(): totals = lax.psum(blocks, 'dp')]
    add x0 -> x4, other arithmetic: none -> 55 us  [shards(): totals + lax.ppermute(totals, 'dp', [(dev, dev ^ hop) for dev in range(16)])]
  transfers between devices with their start and end apart: 3 -> 6, of which waited for: 3 -> 6; matrix products, arithmetic and copies ran while one was open for 1% -> 0% of each run, Pallas kernels for 0% -> 0%
where the time goes in v1:
time: 2150 us; the launch traced here: 2140 us
  waiting for transfers between devices  1690 us (79%)
  other arithmetic  313 us (15%)
  local copies, waits for them, and re-layouts  60.5 us (3%)
  matrix products  59.1 us (3%)
    ppermute x4, waiting for transfers between devices, shards(): lax.ppermute(totals, 'dp', [(dev, dev ^ hop) for dev in range(16)])  1460 us
    all_gather x1, waiting for transfers between devices, shards(): every_rows = lax.all_gather(owner_rows, 'dp', axis=1, tiled=True)  162 us
    another operation x16, other arithmetic, cholesky_basis(): factor = jnp.linalg.cholesky(gram)  154 us
    another operation x4, other arithmetic, cholesky_basis(): lax.linalg.triangular_solve(factor, raw_rows, left_side=False, lower=True...  81.4 us
    all_gather x1, waiting for transfers between devices, shards(): raw_whole = lax.all_gather(raw_proj, 'fsdp', axis=1, tiled=True)  60.9 us
    add x4, other arithmetic, shards(): totals + lax.ppermute(totals, 'dp', [(dev, dev ^ hop) for dev in range(16)])  55 us
  transfers between devices with their start and end apart: 6, of which 6 were waited for; matrix products, arithmetic and copies ran while one was open for 0% of the time, Pallas kernels for 0%

profile of v1, /device:TPU:0, one launch (start us, length us, event | category | flops | bytes accessed | tf_op | source)
XLA Modules:
  0.0 2141.3 jit_solution(14065941936685065880)
XLA Ops:
  7.2 0.7 all-gather.3.cloned.1.call-update
  8.1 60.9 %all-gather.3.cloned.1.call-done = f32[2,1024,512]{2,1,0:T(8,128)} async-done(((f32[2,512,512]{2,1,0:T(8,128)}), f32[2,1024,512]{2,1,0:T(8,128)}) %all-gather.3.cloned.1.call-update) | async-done | bytes 4194320 | tf_op jit(solution)/shard_map/all_gather | solution.py:41
  69.0 10.4 fusion.81
  79.4 1.8 copy.45
  81.2 2.1 fusion.24
  83.3 1.3 copy-done.1
  84.6 23.5 %custom-call.34 = f32[2,128,128]{2,1,0:T(8,128)S(1)} custom-call(f32[2,128,128]{2,1,0:T(8,128)S(1)} %cholesky.274), custom_call_target="Cholesky" | custom-call | tf_op jit(solution)/shard_map/jit(cholesky)/cholesky | solution.py:9
  108.1 19.7 custom-call.35
  127.8 0.3 cholesky.234
  128.1 1.5 constant_dynamic-update-slice_fusion.3
  129.6 1.5 convolution_subtract_fusion.1
  131.1 23.7 %custom-call.36 = f32[2,128,128]{2,1,0:T(8,128)S(1)} custom-call(f32[2,128,128]{2,1,0:T(8,128)S(1)} %cholesky.278), custom_call_target="Cholesky" | custom-call | tf_op jit(solution)/shard_map/jit(cholesky)/cholesky | solution.py:9
  154.8 19.7 custom-call.37
  174.5 0.4 convolution_dynamic-update-slice_fusion
  174.9 1.6 convolution_subtract_fusion.2
  176.4 23.5 %custom-call.38 = f32[2,128,128]{2,1,0:T(8,128)S(1)} custom-call(f32[2,128,128]{2,1,0:T(8,128)S(1)} %cholesky.283), custom_call_target="Cholesky" | custom-call | tf_op jit(solution)/shard_map/jit(cholesky)/cholesky | solution.py:9
  199.9 20.1 custom-call.39
  220.0 0.3 convolution_dynamic-update-slice_fusion.1
  220.3 1.5 convolution_subtract_fusion.3
  221.8 23.5 %custom-call.40 = f32[2,128,128]{2,1,0:T(8,128)S(1)} custom-call(f32[2,128,128]{2,1,0:T(8,128)S(1)} %convolution_subtract_fusion.3), custom_call_target="Cholesky" | custom-call | tf_op jit(solution)/shard_map/jit(cholesky)/cholesky | solution.py:9
  245.3 0.1 compare_reduce_fusion.2
  245.5 0.2 compare_reduce_fusion
  245.7 1.7 select_select_fusion
  247.4 14.2 while.1
  247.5 0.5 fusion.90
  248.0 3.0 bitcast_dynamic-update-slice_fusion.2
  251.1 0.5 fusion.90
  251.6 3.0 bitcast_dynamic-update-slice_fusion.2
  254.6 0.5 fusion.90
  255.2 3.0 bitcast_dynamic-update-slice_fusion.2
  258.2 0.5 fusion.90
  258.8 2.9 bitcast_dynamic-update-slice_fusion.2
  261.7 79.6 %custom-call.41 = f32[2,4,128,128]{2,3,1,0:T(8,128)S(1)} custom-call(f32[2,4,128,128]{3,2,1,0:T(8,128)} %bitcast.134), custom_call_target="InvertDiagBlocksLowerTriangular" | custom-call | tf_op jit(solution)/shard_map/triangular_solve | solution.py:10
  341.3 2.3 bitcast_convert_fusion
  343.6 3.2 convolution_subtract_fusion
  346.8 1.1 fusion.80
  347.9 4.6 fusion.30
  352.5 1.1 fusion.79
  353.6 6.5 fusion.33
  360.2 1.1 convolution_convert_fusion
  361.3 15.9 fusion.2
  377.2 17.5 copy.60
  394.7 25.5 %collective-permute-done = f32[2,256,16,512]{3,2,1,0:T(8,128)} collective-permute-done((f32[2,256,16,512]{3,2,1,0:T(8,128)}, f32[2,256,16,512]{3,2,1,0:T(8,128)}, u32[]{:S(2)}, u32[]{:S(2)}) %collective-permute-start) | collective-permute-done | bytes 16777248 | tf_op jit(solution)/shard_map/ppermute | solution.py:59
  420.1 11.9 add.100
  432.0 1.5 collective-permute-start.1
  433.6 360.9 %collective-permute-done.1 = f32[2,256,16,512]{3,2,1,0:T(8,128)} collective-permute-done((f32[2,256,16,512]{3,2,1,0:T(8,128)S(1)}, f32[2,256,16,512]{3,2,1,0:T(8,128)}, u32[]{:S(2)}, u32[]{:S(2)}) %collective-permute-start.1) | collective-permute-done | bytes 16777248 | tf_op jit(solution)/shard_map/ppermute | solution.py:59
  794.5 12.7 add.101
  807.2 1.5 collective-permute-start.2
  808.7 360.1 %collective-permute-done.2 = f32[2,256,16,512]{3,2,1,0:T(8,128)S(1)} collective-permute-done((f32[2,256,16,512]{3,2,1,0:T(8,128)}, f32[2,256,16,512]{3,2,1,0:T(8,128)S(1)}, u32[]{:S(2)}, u32[]{:S(2)}) %collective-permute-start.2) | collective-permute-done | bytes 16777248 | tf_op jit(solution)/shard_map/ppermute | solution.py:59
  1168.8 12.7 add.102
  1181.6 2.4 collective-permute-start.3
  1184.0 0.2 convert_reduce_fusion
  1184.3 0.2 select_reduce_fusion
  1184.8 718.1 %collective-permute-done.3 = f32[2,256,16,512]{3,2,1,0:T(8,128)} collective-permute-done((f32[2,256,16,512]{3,2,1,0:T(8,128)}, f32[2,256,16,512]{3,2,1,0:T(8,128)}, u32[]{:S(2)}, u32[]{:S(2)}) %collective-permute-start.3) | collective-permute-done | bytes 16777248 | tf_op jit(solution)/shard_map/ppermute | solution.py:59
  1902.9 17.6 add.103
  1920.5 6.5 gather_fusion
  1927.0 6.2 fusion.27
  1933.2 0.1 broadcast_in_dim.58
  1933.3 0.2 broadcast_in_dim.59
  1933.5 0.2 fusion.46
  1933.8 5.2 fusion.17
  1939.0 162.3 %all-gather.5.cloned.1.call-done = bf16[2,512,16,1024]{3,2,1,0:T(8,128)(2,1)} async-done(((bf16[2,32,16,1024]{3,2,1,0:T(8,128)(2,1)}), bf16[2,512,16,1024]{3,2,1,0:T(8,128)(2,1)}) %all-gather.5.cloned.1.call-update) | async-done | bytes 33554448 | tf_op jit(solution)/shard_map/all_gather | solution.py:71
  2101.3 18.4 gather_fusion.1
  2119.7 14.2 bitcast_select_fusion
  (39 shorter events, 1.1 us)
Async XLA Ops:
  7.2 61.8 %all-gather.3.cloned.1.call-start = ((), (), s32[]{:S(2)}) async-start(), calls=%async_computation | async-start | bytes 6291456 | tf_op jit(solution)/shard_map/all_gather | solution.py:41
  7.9 2093.4 %all-gather.5.cloned.1.call-start = ((), (), s32[]{:S(2)}) async-start(), calls=%async_computation.1 | async-start | bytes 35651584 | tf_op jit(solution)/shard_map/all_gather | solution.py:71
  83.3 1.3 copy-start.1
  343.5 4.4 copy-start
  347.9 13.4 copy-start.2
  353.6 7.7 copy-start.3
  394.6 25.5 %collective-permute-start = (f32[2,256,16,512]{3,2,1,0:T(8,128)}, f32[2,256,16,512]{3,2,1,0:T(8,128)}, u32[]{:S(2)}, u32[]{:S(2)}) collective-permute-start(f32[2,256,16,512]{3,2,1,0:T(8,128)} %bitcast.126), channel_id=1, source_target_pairs={{0,2},{2,0},{4,6},{6,4},{8,10},{10,8},{12,14},{14,12},{16,18},{18,... | collective-permute-start | bytes 50331656 | tf_op jit(solution)/shard_map/ppermute | solution.py:59
  432.0 362.4 %collective-permute-start.1 = (f32[2,256,16,512]{3,2,1,0:T(8,128)S(1)}, f32[2,256,16,512]{3,2,1,0:T(8,128)}, u32[]{:S(2)}, u32[]{:S(2)}) collective-permute-start(f32[2,256,16,512]{3,2,1,0:T(8,128)S(1)} %add.100), channel_id=1, source_target_pairs={{0,4},{2,6},{4,0},{6,2},{8,12},{10,14},{12,8},{14,10},{16,20},{18,... | collective-permute-start | bytes 50331656 | tf_op jit(solution)/shard_map/ppermute | solution.py:59
  807.2 376.8 %copy-start.4 = (s32[2,256]{1,0:T(2,128)S(1)}, s32[2,256]{1,0:T(2,128)}, u32[]{:S(2)}) copy-start(s32[2,256]{1,0:T(2,128)} %param.7) | copy-start | bytes 6148
  807.2 361.6 %collective-permute-start.2 = (f32[2,256,16,512]{3,2,1,0:T(8,128)}, f32[2,256,16,512]{3,2,1,0:T(8,128)S(1)}, u32[]{:S(2)}, u32[]{:S(2)}) collective-permute-start(f32[2,256,16,512]{3,2,1,0:T(8,128)} %add.101), channel_id=1, source_target_pairs={{0,8},{2,10},{4,12},{6,14},{8,0},{10,2},{12,4},{14,6},{16,24},{18,... | collective-permute-start | bytes 50331656 | tf_op jit(solution)/shard_map/ppermute | solution.py:59
  1181.6 721.3 %collective-permute-start.3 = (f32[2,256,16,512]{3,2,1,0:T(8,128)}, f32[2,256,16,512]{3,2,1,0:T(8,128)}, u32[]{:S(2)}, u32[]{:S(2)}) collective-permute-start(f32[2,256,16,512]{3,2,1,0:T(8,128)} %add.102), channel_id=1, source_target_pairs={{0,16},{2,18},{4,20},{6,22},{8,24},{10,26},{12,28},{14,30},{16,0},... | collective-permute-start | bytes 50331656 | tf_op jit(solution)/shard_map/ppermute | solution.py:59
Sparse Core Ops, SparseCore 0:
  9.5 59.4 all-gather.2
  1933.3 167.9 all-gather.4
